TPU v7x, 32 devices: a whole 2x2x4 slice. The times are simulated.
32 devices in a mesh: grp: 8 (over z, y), tm: 4 (over x, core).
Axes of the slice: x: 2, y: 2, z: 4, core: 2. Of those that a mesh axis runs over, the one named last changes fastest.
Arguments:
- voltages: bfloat16 [2, 192, 1048576], P(None, 'grp', 'tm'), may hold values from -6 to 6
- filter_taps: float32 [4, 4096], replicated, may hold values from -3 to 3
- delays: int32 [192, 1536], replicated, may hold values from 0 to 4095
- shifts: int32 [4, 512], replicated, may hold values from 0 to 2
Outputs:
- dedispersed: float32 [1536, 512, 32], P('grp', None, 'tm')
All inputs are finite; a program needn't handle non-finite values.
Results may differ from a plain program's by a relative error of at most 0.0014.
Values may be sent and summed in bfloat16 or wider, within the bound.
No kernel may reach another device: no remote copies, remote signals or barrier semaphores. Data moves between devices by JAX's collectives and lax.ppermute only.
A program may use at most 192 MiB of HBM per device.

v0:
```python
import math
import jax
import jax.numpy as jnp
from jax import lax
from jax.sharding import PartitionSpec as P

STATIONS = 192
TRANSFORM = 4096
CHANNELS = 512
TAPS = 4
INTEG = 8
LEVELS = 4
SHIFT_MOST = 2
two_pi = 2.0 * math.pi


def from_behind(x, axis, by):
    length = lax.axis_size(axis)
    pairs = [(i, i + by) for i in range(length) if 0 <= i + by < length]
    return lax.ppermute(x, axis, pairs)


def for_sending(x):
    return jax.tree.map(lambda a: a.astype(jnp.bfloat16) if a.dtype == jnp.float32 else a, x)


def dft_tables():
    rows_index = jnp.arange(CHANNELS, dtype=jnp.int32)
    cols_index = jnp.arange(TRANSFORM, dtype=jnp.int32)
    product = rows_index[:, None] * cols_index[None, :] % TRANSFORM
    angles = product.astype(jnp.float32) * (two_pi / TRANSFORM)
    scaling = 1.0 / math.sqrt(TRANSFORM)
    return (
        (jnp.cos(angles) * scaling).astype(jnp.bfloat16),
        (jnp.sin(angles) * scaling).astype(jnp.bfloat16),
    )


def beam_weights(channel, delays):
    phases = (channel * delays.T % TRANSFORM).astype(jnp.float32) * (two_pi / TRANSFORM)
    scaling = 1.0 / math.sqrt(STATIONS)
    return (
        (jnp.cos(phases) * scaling).astype(jnp.bfloat16),
        (jnp.sin(phases) * scaling).astype(jnp.bfloat16),
    )


def to_spectra(filtered, cosine, sine):
    real_part = jnp.einsum(
        "kn,stn->kst", cosine, filtered[0], preferred_element_type=jnp.float32
    ) + jnp.einsum("kn,stn->kst", sine, filtered[1], preferred_element_type=jnp.float32)
    imag_part = jnp.einsum(
        "kn,stn->kst", cosine, filtered[1], preferred_element_type=jnp.float32
    ) - jnp.einsum("kn,stn->kst", sine, filtered[0], preferred_element_type=jnp.float32)
    spectra = jnp.stack([real_part, imag_part]).astype(jnp.bfloat16)
    return spectra.reshape(2, CHANNELS, spectra.shape[2], -1, INTEG)


def dedisperse_level(leading, trailing, amounts, out_len):
    shifted = jnp.zeros(leading.shape[:3] + (2, out_len), jnp.float32)
    for offset in range(SHIFT_MOST + 1):
        selector = (amounts == offset).astype(jnp.float32)[None, :, :, :, None]
        shifted = shifted + selector * trailing[:, :, :, None, offset : offset + out_len]
    combined = 0.5 * (leading[:, :, :, None, :] + shifted)
    return combined.reshape(leading.shape[0], -1, out_len)


def local(voltages, filter_taps, delays, shifts):
    station_count = voltages.shape[1]
    frames = voltages.shape[2] // TRANSFORM
    framed = voltages.reshape(2, station_count, frames, TRANSFORM)
    last_frames = framed[:, :, frames - (TAPS - 1) :, :]
    previous = from_behind(last_frames, "tm", 1)
    extended = jnp.concatenate([previous, framed], axis=2).astype(jnp.float32)
    filtered = jnp.zeros((2, station_count, frames, TRANSFORM), jnp.float32)
    for tap in range(TAPS):
        start = TAPS - 1 - tap
        filtered = (
            filtered
            + filter_taps[tap][None, None, None, :] * extended[:, :, start : start + frames, :]
        )
    filtered = filtered.astype(jnp.bfloat16)
    cosine, sine = dft_tables()
    local_channels = CHANNELS // lax.axis_size("grp")
    spectra_all = to_spectra(filtered, cosine, sine)
    received = lax.all_to_all(spectra_all, "grp", split_axis=1, concat_axis=2, tiled=True)
    item_count = received.shape[3]
    all_stations = received.shape[2]
    spectra = received.reshape(2, local_channels, all_stations, item_count * INTEG)
    first_channel = lax.axis_index("grp") * local_channels

    def channel_powers(local_index):
        channel_data = lax.dynamic_index_in_dim(spectra, local_index, 1, keepdims=False)
        weight_cos, weight_sin = beam_weights(first_channel + local_index, delays)
        beam_real = jnp.dot(
            weight_cos, channel_data[0], preferred_element_type=jnp.float32
        ) + jnp.dot(weight_sin, channel_data[1], preferred_element_type=jnp.float32)
        beam_imag = jnp.dot(
            weight_cos, channel_data[1], preferred_element_type=jnp.float32
        ) - jnp.dot(weight_sin, channel_data[0], preferred_element_type=jnp.float32)
        energy = beam_real * beam_real + beam_imag * beam_imag
        power = energy.reshape(energy.shape[0], item_count, INTEG).sum(axis=-1) * (1.0 / INTEG)
        return power.astype(jnp.bfloat16)

    powers = lax.map(channel_powers, jnp.arange(local_channels, dtype=jnp.int32))
    powers = jnp.transpose(powers, (1, 0, 2))
    owned = lax.all_to_all(powers, "grp", split_axis=0, concat_axis=1, tiled=True)
    current = owned.astype(jnp.float32)
    beam_count = current.shape[0]
    power_len = current.shape[2]
    for level_index in range(1, LEVELS + 1):
        half_width = 2 ** (level_index - 1)
        group_count = CHANNELS // (2 * half_width)
        grouped = current.reshape(beam_count, group_count, 2, half_width, power_len)
        leading = grouped[:, :, 0]
        trailing_own = grouped[:, :, 1]
        next_rim = from_behind(for_sending(trailing_own[:, :, :, :SHIFT_MOST]), "tm", -1)
        trailing = jnp.concatenate([trailing_own, next_rim], axis=3)
        amounts = shifts[level_index - 1].reshape(group_count, half_width, 2)
        current = dedisperse_level(leading, trailing, amounts, power_len)
    return current


def solution(mesh):
    placed = (P(None, "grp", "tm"), P(), P(), P())
    return jax.shard_map(
        local, mesh=mesh, in_specs=placed, out_specs=P("grp", None, "tm"), check_vma=False
    )
```

profile of v0, /device:TPU:1, one launch (start us, length us, event | category | flops | bytes accessed | tf_op | source)
XLA Modules:
  0.0 1462.5 jit_solution(16832688132228220939)
XLA Ops:
  0.0 21.3 %copy.154 = bf16[6,8,64,4096]{3,2,1,0:T(8,128)(2,1)S(1)} copy(bf16[6,8,64,4096]{3,1,2,0:T(8,128)(2,1)} %bitcast.195) | data formatting | bytes 50331648
  27.7 13.1 collective-permute-done
  41.8 19.4 %maximum_convert_fusion = f32[2,24,67,4096]{3,2,1,0:T(8,128)} fusion(bf16[2,24,64,4096]{3,2,1,0:T(8,128)(2,1)S(1)} %bitcast.192, bf16[2,24,3,4096]{3,2,1,0:T(4,128)(2,1)S(1)} %copy.126), kind=kLoop, calls=%fused_computation.34 | loop fusion | flops 52690944 | bytes 79036416 | tf_op jit(solution)/shard_map/convert_element_type | solution.py:74
  61.1 76.4 %fusion.17 = bf16[2,24,64,4096]{3,2,1,0:T(8,128)(2,1)} fusion(f32[2,24,67,4096]{3,2,1,0:T(8,128)} %maximum_convert_fusion, f32[4096]{0:T(1024)S(1)} %bitcast.215, f32[4096]{0:T(1024)S(1)} %bitcast.216, f32[4096]{0:T(1024)S(1)} %bitcast.214, f32[4096]{0:T(1024)S(1)} %bitcast.213), kind=kLoop, calls=%fused_computation.28 | loop fusion | flops 100663296 | bytes 226557952 | tf_op jit(solution)/shard_map/convert_element_type | solution.py:82
  137.5 43.1 %fusion.23 = f32[512,24,64]{0,2,1:T(8,128)} fusion(bf16[2,24,64,4096]{3,2,1,0:T(8,128)(2,1)} %fusion.17), kind=kOutput, calls=%fused_computation.43 | convolution fusion | flops 6476005376 | bytes 15728640 | tf_op jit(solution)/shard_map/kn,stn->kst/dot_general | solution.py:51
  180.7 42.4 %fusion.20 = f32[512,24,64]{0,2,1:T(8,128)S(1)} fusion(bf16[2,24,64,4096]{3,2,1,0:T(8,128)(2,1)} %fusion.17), kind=kOutput, calls=%fused_computation.40 | convolution fusion | flops 6476005376 | bytes 15728640 | tf_op jit(solution)/shard_map/kn,stn->kst/dot_general | solution.py:54
  223.1 43.9 %fusion.48 = bf16[1,512,24,8,8]{1,4,3,2,0:T(8,128)(2,1)S(1)} fusion(f32[512,24,64]{0,2,1:T(8,128)} %fusion.23, bf16[2,24,64,4096]{3,2,1,0:T(8,128)(2,1)} %fusion.17), kind=kOutput, calls=%fused_computation.89 | convolution fusion | flops 6477578240 | bytes 17301504 | tf_op jit(solution)/shard_map/kn,stn->kst/dot_general | solution.py:49
  266.9 41.9 %fusion.51 = bf16[1,512,24,8,8]{1,4,3,2,0:T(8,128)(2,1)S(1)} fusion(f32[512,24,64]{0,2,1:T(8,128)S(1)} %fusion.20, bf16[2,24,64,4096]{3,2,1,0:T(8,128)(2,1)} %fusion.17), kind=kOutput, calls=%fused_computation.90 | convolution fusion | flops 6477578240 | bytes 17301504 | tf_op jit(solution)/shard_map/kn,stn->kst/dot_general | solution.py:52
  309.1 26.3 %copy.127 = bf16[2,512,24,8,8]{2,4,3,0,1:T(8,128)(2,1)} copy(bf16[2,512,24,8,8]{1,4,3,2,0:T(8,128)(2,1)S(1)} %pad_maximum_fusion) | data formatting | bytes 6291456 | tf_op jit(solution)/shard_map/stack | solution.py:55
  335.5 24.2 %reshape.336 = bf16[8,2,98304]{2,1,0:T(2,128)(2,1)} reshape(bf16[512,2,8,8,24]{4,3,2,1,0:T(8,128)(2,1)} %bitcast.193) | data formatting | bytes 6291456
  359.7 5.8 all-to-all-start
  365.5 60.2 %all-to-all-done = bf16[8,2,98304]{2,1,0:T(2,128)(2,1)S(1)} async-done(((bf16[8,2,98304]{2,1,0:T(2,128)(2,1)}), bf16[8,2,98304]{2,1,0:T(2,128)(2,1)S(1)}, u32[]{:S(2)}, u32[]{:S(2)}) %all-to-all-start) | async-done | bytes 3145760 | tf_op jit(solution)/shard_map/all_to_all | solution.py:86
  425.8 25.3 %reshape.337 = bf16[512,2,8,8,24]{4,3,2,1,0:T(8,128)(2,1)} reshape(bf16[8,2,98304]{2,1,0:T(2,128)(2,1)S(1)} %all-to-all-done) | data formatting | bytes 6291456
  451.1 25.2 %copy.129 = bf16[2,64,8,24,8,8]{1,5,4,3,2,0:T(8,128)(2,1)} copy(bf16[2,64,8,24,8,8]{3,5,4,0,1,2:T(8,128)(2,1)} %bitcast.194) | data formatting | bytes 6291456 | tf_op jit(solution)/shard_map/all_to_all | solution.py:86
  476.3 9.6 copy.130
  485.9 832.3 %while.12 = (s32[]{:T(128)}, bf16[64,1536,8]{1,2,0:T(8,128)(2,1)}, s32[64]{0:T(128)S(1)}, s32[]{:T(128)}, s32[192,1536]{1,0:T(8,128)S(1)}, /*index=5*/bf16[2,64,...) while((s32[]{:T(128)}, bf16[64,1536,8]{1,2,0:T(8,128)(2,1)}, s32[64]{0:T(128)S(1)}, s32[]{:T(128)}, ...), condition=%wide.region_2.3_spmd, body=%wide.region_0.2_spmd.sunk | while | flops 156905472 | bytes 7398087 | solution.py:105
  489.1 4.8 multiply_convert_fusion.6
  502.1 4.8 multiply_convert_fusion.6
  515.1 4.8 multiply_convert_fusion.6
  528.1 4.8 multiply_convert_fusion.6
  541.1 4.8 multiply_convert_fusion.6
  554.1 4.8 multiply_convert_fusion.6
  567.1 4.8 multiply_convert_fusion.6
  580.1 4.8 multiply_convert_fusion.6
  593.1 4.8 multiply_convert_fusion.6
  606.1 4.8 multiply_convert_fusion.6
  619.2 4.8 multiply_convert_fusion.6
  632.2 4.8 multiply_convert_fusion.6
  645.2 4.8 multiply_convert_fusion.6
  658.2 4.8 multiply_convert_fusion.6
  671.2 4.8 multiply_convert_fusion.6
  684.2 4.8 multiply_convert_fusion.6
  697.2 4.8 multiply_convert_fusion.6
  710.2 4.8 multiply_convert_fusion.6
  723.2 4.8 multiply_convert_fusion.6
  736.2 4.8 multiply_convert_fusion.6
  749.2 4.8 multiply_convert_fusion.6
  762.2 4.8 multiply_convert_fusion.6
  775.2 4.8 multiply_convert_fusion.6
  788.2 4.8 multiply_convert_fusion.6
  801.2 4.8 multiply_convert_fusion.6
  814.2 4.8 multiply_convert_fusion.6
  827.3 4.8 multiply_convert_fusion.6
  840.3 4.8 multiply_convert_fusion.6
  853.3 4.8 multiply_convert_fusion.6
  866.3 4.8 multiply_convert_fusion.6
  879.3 4.8 multiply_convert_fusion.6
  892.3 4.8 multiply_convert_fusion.6
  905.3 4.8 multiply_convert_fusion.6
  918.3 4.8 multiply_convert_fusion.6
  931.3 4.8 multiply_convert_fusion.6
  944.3 4.8 multiply_convert_fusion.6
  970.3 4.8 multiply_convert_fusion.6
  983.3 4.8 multiply_convert_fusion.6
  996.3 4.8 multiply_convert_fusion.6
  1152.4 4.8 multiply_convert_fusion.6
  1243.4 4.8 multiply_convert_fusion.6
  1256.4 4.8 multiply_convert_fusion.6
  1324.5 5.8 reshape.338
  1330.3 38.8 %all_to_all.24 = bf16[8,2,49152]{2,1,0:T(2,128)(2,1)} all-to-all(bf16[8,2,49152]{2,1,0:T(2,128)(2,1)S(1)} %reshape.338), channel_id=1, replica_groups=mesh['grp'=8,'tm'=4] {'grp'}, dimensions={0} | all-to-all | bytes 3145728 | tf_op jit(solution)/shard_map/all_to_all | solution.py:107
  1369.1 5.2 reshape.339
  1432.3 5.4 collective-permute-done.3
  1446.8 5.1 collective-permute-done.4
  1456.8 5.2 copy.148
  (492 shorter events, 546.7 us)
Async XLA Ops:
  21.3 6.4 copy-start.6
  23.1 17.6 %collective-permute-start = (bf16[2,24,3,4096]{3,1,2,0:T(8,128)(2,1)S(1)}, bf16[2,24,3,4096]{3,1,2,0:T(8,128)(2,1)S(1)}, u32[]{:S(2)}, u32[]{:S(2)}) collective-permute-start(bf16[2,24,3,4096]{3,1,2,0:T(8,128)(2,1)S(1)} %copy.125), channel_id=1, source_target_pairs={{0,1},{1,2},{2,3},{4,5},{5,6},{6,7},{8,9},{9,10},{10,11},{12,13},{... | collective-permute-start | bytes 3538952 | tf_op jit(solution)/shard_map/ppermute | solution.py:20
  359.7 66.0 %all-to-all-start = ((bf16[8,2,98304]{2,1,0:T(2,128)(2,1)}), bf16[8,2,98304]{2,1,0:T(2,128)(2,1)S(1)}, u32[]{:S(2)}, u32[]{:S(2)}) async-start(bf16[8,2,98304]{2,1,0:T(2,128)(2,1)} %reshape.336), calls=%async_computation | async-start | bytes 6291456 | tf_op jit(solution)/shard_map/all_to_all | solution.py:86
  476.3 9.6 copy-start
  1378.3 8.6 copy-start.7
  1385.0 8.0 collective-permute-start.1
  1390.0 3.0 copy-start.5
  1406.6 7.1 collective-permute-start.2
  1421.9 1.6 copy-start.3
  1422.3 1.9 copy-start.2
  1423.9 1.7 copy-start.1
  1430.0 7.7 collective-permute-start.3
  1439.2 1.6 copy-start.4
  1444.2 7.7 collective-permute-start.4
where the time goes:
time: 1480 us; the launch traced here: 1460 us
  other arithmetic  464 us (31%)
  matrix products  449 us (30%)
  local copies, waits for them, and re-layouts  238 us (16%)
  loops' own time  168 us (11%)
  waiting for transfers between devices  84.6 us (6%)
  blocking collectives  38.8 us (3%)
  starting transfers between devices  18 us (1%)
    convert_element_type x64, other arithmetic, beam_weights(): (jnp.sin(phases) * scaling).astype(jnp.bfloat16)  309 us
    another operation x1, loops' own time, local(): lax.map(channel_powers, jnp.arange(local_channels, dtype=jnp.int32))  168 us
    unnamed x23, local copies, waits for them, and re-layouts  89.1 us
    convert_element_type x1, other arithmetic, local(): filtered = filtered.astype(jnp.bfloat16)  76.4 us
    dot_general x64, matrix products, channel_powers(): jnp.dot(weight_sin, channel_data[0], preferred_element_type=jnp.float32)  73 us
    dot_general x64, matrix products, channel_powers(): jnp.dot(weight_sin, channel_data[1], preferred_element_type=jnp.float32)  68.7 us
    dot_general x64, matrix products, channel_powers(): jnp.dot(weight_cos, channel_data[1], preferred_element_type=jnp.float32)  68.3 us
    dot_general x64, matrix products, channel_powers(): jnp.dot(weight_cos, channel_data[0], preferred_element_type=jnp.float32)  68.2 us
  transfers between devices with their start and end apart: 6, of which 5 were waited for; matrix products, arithmetic and copies ran while one was open for 1% of the time, Pallas kernels for 0%

commit v1 on v0

--- a/solution.py
+++ b/solution.py
@@ -83,7 +83,9 @@
     cosine, sine = dft_tables()
     local_channels = CHANNELS // lax.axis_size("grp")
     spectra_all = to_spectra(filtered, cosine, sine)
-    received = lax.all_to_all(spectra_all, "grp", split_axis=1, concat_axis=2, tiled=True)
+    shards = jnp.split(spectra_all, lax.axis_size("grp"), axis=1)
+    got = lax.all_to_all(jnp.stack(shards), "grp", 0, 0)
+    received = jnp.concatenate(got, axis=2)
     item_count = received.shape[3]
     all_stations = received.shape[2]
     spectra = received.reshape(2, local_channels, all_stations, item_count * INTEG)

time: 1480 us -> 1410 us (0.953)
  local copies, waits for them, and re-layouts: 238 us -> 163 us
    unnamed x23, local copies, waits for them, and re-layouts: 89.1 us -> 57.3 us
    another operation x1 -> x0, local copies, waits for them, and re-layouts: 26.3 us -> none  [to_spectra(): spectra = jnp.stack([real_part, imag_part]).astype(jnp.bfloat16)]
    all_to_all x1 -> x0, local copies, waits for them, and re-layouts: 25.2 us -> none  [local(): lax.all_to_all(spectra_all, 'grp', split_axis=1, concat_axis=2, tiled=True)]
where the time goes in v1:
time: 1410 us; the launch traced here: 1390 us
  other arithmetic  469 us (33%)
  matrix products  449 us (32%)
  loops' own time  168 us (12%)
  local copies, waits for them, and re-layouts  163 us (12%)
  waiting for transfers between devices  84.6 us (6%)
  blocking collectives  38.8 us (3%)
  starting transfers between devices  17.7 us (1%)
    convert_element_type x64, other arithmetic, beam_weights(): (jnp.sin(phases) * scaling).astype(jnp.bfloat16)  309 us
    another operation x1, loops' own time, local(): lax.map(channel_powers, jnp.arange(local_channels, dtype=jnp.int32))  168 us
    convert_element_type x1, other arithmetic, local(): filtered = filtered.astype(jnp.bfloat16)  76.4 us
    dot_general x64, matrix products, channel_powers(): jnp.dot(weight_sin, channel_data[0], preferred_element_type=jnp.float32)  73 us
    dot_general x64, matrix products, channel_powers(): jnp.dot(weight_sin, channel_data[1], preferred_element_type=jnp.float32)  68.7 us
    dot_general x64, matrix products, channel_powers(): jnp.dot(weight_cos, channel_data[1], preferred_element_type=jnp.float32)  68.3 us
    dot_general x64, matrix products, channel_powers(): jnp.dot(weight_cos, channel_data[0], preferred_element_type=jnp.float32)  68.2 us
    all_to_all x1, waiting for transfers between devices, local(): got = lax.all_to_all(jnp.stack(shards), 'grp', 0, 0)  60.3 us
  transfers between devices with their start and end apart: 6, of which 5 were waited for; matrix products, arithmetic and copies ran while one was open for 1% of the time, Pallas kernels for 0%

profile of v1, /device:TPU:1, one launch (start us, length us, event | category | flops | bytes accessed | tf_op | source)
XLA Modules:
  0.0 1391.4 jit_solution(970233014241460200)
XLA Ops:
  0.0 21.3 %copy.153 = bf16[6,8,64,4096]{3,2,1,0:T(8,128)(2,1)S(1)} copy(bf16[6,8,64,4096]{3,1,2,0:T(8,128)(2,1)} %bitcast.224) | data formatting | bytes 50331648
  27.7 13.1 collective-permute-done
  41.8 19.4 %maximum_convert_fusion = f32[2,24,67,4096]{3,2,1,0:T(8,128)} fusion(bf16[2,24,64,4096]{3,2,1,0:T(8,128)(2,1)S(1)} %bitcast.223, bf16[2,24,3,4096]{3,2,1,0:T(4,128)(2,1)S(1)} %copy.129), kind=kLoop, calls=%fused_computation.34 | loop fusion | flops 52690944 | bytes 79036416 | tf_op jit(solution)/shard_map/convert_element_type | solution.py:74
  61.1 76.4 %fusion.17 = bf16[2,24,64,4096]{3,2,1,0:T(8,128)(2,1)} fusion(f32[2,24,67,4096]{3,2,1,0:T(8,128)} %maximum_convert_fusion, f32[4096]{0:T(1024)S(1)} %bitcast.245, f32[4096]{0:T(1024)S(1)} %bitcast.246, f32[4096]{0:T(1024)S(1)} %bitcast.244, f32[4096]{0:T(1024)S(1)} %bitcast.243), kind=kLoop, calls=%fused_computation.28 | loop fusion | flops 100663296 | bytes 226557952 | tf_op jit(solution)/shard_map/convert_element_type | solution.py:82
  137.5 43.1 %fusion.20 = f32[512,24,64]{0,2,1:T(8,128)} fusion(bf16[2,24,64,4096]{3,2,1,0:T(8,128)(2,1)} %fusion.17), kind=kOutput, calls=%fused_computation.40 | convolution fusion | flops 6476005376 | bytes 15728640 | tf_op jit(solution)/shard_map/kn,stn->kst/dot_general | solution.py:54
  180.7 42.4 %fusion.23 = f32[512,24,64]{0,2,1:T(8,128)S(1)} fusion(bf16[2,24,64,4096]{3,2,1,0:T(8,128)(2,1)} %fusion.17), kind=kOutput, calls=%fused_computation.43 | convolution fusion | flops 6476005376 | bytes 15728640 | tf_op jit(solution)/shard_map/kn,stn->kst/dot_general | solution.py:51
  223.1 43.9 %fusion.51 = bf16[1,512,24,8,8]{1,4,3,2,0:T(8,128)(2,1)S(1)} fusion(f32[512,24,64]{0,2,1:T(8,128)} %fusion.20, bf16[2,24,64,4096]{3,2,1,0:T(8,128)(2,1)} %fusion.17), kind=kOutput, calls=%fused_computation.103 | convolution fusion | flops 6477578240 | bytes 17301504 | tf_op jit(solution)/shard_map/kn,stn->kst/dot_general | solution.py:52
  266.9 41.9 %fusion.48 = bf16[1,512,24,8,8]{1,4,3,2,0:T(8,128)(2,1)S(1)} fusion(f32[512,24,64]{0,2,1:T(8,128)S(1)} %fusion.23, bf16[2,24,64,4096]{3,2,1,0:T(8,128)(2,1)} %fusion.17), kind=kOutput, calls=%fused_computation.102 | convolution fusion | flops 6477578240 | bytes 17301504 | tf_op jit(solution)/shard_map/kn,stn->kst/dot_general | solution.py:49
  314.4 8.9 reshape.335
  323.3 5.5 all-to-all-start
  328.9 60.3 %all-to-all-done = bf16[8,2,98304]{2,1,0:T(2,128)(2,1)S(1)} async-done(((bf16[8,2,98304]{2,1,0:T(2,128)(2,1)}), bf16[8,2,98304]{2,1,0:T(2,128)(2,1)S(1)}, u32[]{:S(2)}, u32[]{:S(2)}) %all-to-all-start) | async-done | bytes 3145760 | tf_op jit(solution)/shard_map/all_to_all | solution.py:87
  389.2 6.2 reshape.336
  403.8 9.6 copy.131
  413.4 832.4 %while.12 = (s32[]{:T(128)}, bf16[64,1536,8]{1,2,0:T(8,128)(2,1)}, s32[64]{0:T(128)S(1)}, s32[]{:T(128)}, s32[192,1536]{1,0:T(8,128)S(1)}, /*index=5*/bf16[2,64,...) while((s32[]{:T(128)}, bf16[64,1536,8]{1,2,0:T(8,128)(2,1)}, s32[64]{0:T(128)S(1)}, s32[]{:T(128)}, ...), condition=%wide.region_2.3_spmd, body=%wide.region_0.2_spmd.sunk | while | flops 156905472 | bytes 7398087 | solution.py:107
  416.6 4.8 multiply_convert_fusion.6
  429.6 4.8 multiply_convert_fusion.6
  442.6 4.8 multiply_convert_fusion.6
  455.6 4.8 multiply_convert_fusion.6
  468.6 4.8 multiply_convert_fusion.6
  481.7 4.8 multiply_convert_fusion.6
  494.7 4.8 multiply_convert_fusion.6
  507.7 4.8 multiply_convert_fusion.6
  520.7 4.8 multiply_convert_fusion.6
  533.7 4.8 multiply_convert_fusion.6
  546.7 4.8 multiply_convert_fusion.6
  559.7 4.8 multiply_convert_fusion.6
  572.7 4.8 multiply_convert_fusion.6
  585.7 4.8 multiply_convert_fusion.6
  598.7 4.8 multiply_convert_fusion.6
  611.7 4.8 multiply_convert_fusion.6
  624.7 4.8 multiply_convert_fusion.6
  637.7 4.8 multiply_convert_fusion.6
  650.8 4.8 multiply_convert_fusion.6
  663.8 4.8 multiply_convert_fusion.6
  676.8 4.8 multiply_convert_fusion.6
  689.8 4.8 multiply_convert_fusion.6
  702.8 4.8 multiply_convert_fusion.6
  715.8 4.8 multiply_convert_fusion.6
  728.8 4.8 multiply_convert_fusion.6
  741.8 4.8 multiply_convert_fusion.6
  754.8 4.8 multiply_convert_fusion.6
  767.8 4.8 multiply_convert_fusion.6
  780.8 4.8 multiply_convert_fusion.6
  793.8 4.8 multiply_convert_fusion.6
  806.8 4.8 multiply_convert_fusion.6
  819.8 4.8 multiply_convert_fusion.6
  832.8 4.8 multiply_convert_fusion.6
  845.8 4.8 multiply_convert_fusion.6
  858.8 4.8 multiply_convert_fusion.6
  871.8 4.8 multiply_convert_fusion.6
  884.8 4.8 multiply_convert_fusion.6
  897.9 4.8 multiply_convert_fusion.6
  949.9 4.8 multiply_convert_fusion.6
  962.9 4.8 multiply_convert_fusion.6
  1001.9 4.8 multiply_convert_fusion.6
  1027.9 4.8 multiply_convert_fusion.6
  1053.9 4.8 multiply_convert_fusion.6
  1080.0 4.8 multiply_convert_fusion.6
  1252.1 5.8 reshape.337
  1257.9 38.8 %all_to_all.14 = bf16[8,2,49152]{2,1,0:T(2,128)(2,1)} all-to-all(bf16[8,2,49152]{2,1,0:T(2,128)(2,1)S(1)} %reshape.337), channel_id=1, replica_groups=mesh['grp'=8,'tm'=4] {'grp'}, dimensions={0} | all-to-all | bytes 3145728 | tf_op jit(solution)/shard_map/all_to_all | solution.py:109
  1296.7 5.2 reshape.338
  1361.4 5.4 collective-permute-done.3
  1375.9 5.1 collective-permute-done.4
  1386.0 5.2 copy.149
  (499 shorter events, 552.3 us)
Async XLA Ops:
  21.3 6.4 copy-start.6
  23.1 17.6 %collective-permute-start = (bf16[2,24,3,4096]{3,1,2,0:T(8,128)(2,1)S(1)}, bf16[2,24,3,4096]{3,1,2,0:T(8,128)(2,1)S(1)}, u32[]{:S(2)}, u32[]{:S(2)}) collective-permute-start(bf16[2,24,3,4096]{3,1,2,0:T(8,128)(2,1)S(1)} %copy.128), channel_id=1, source_target_pairs={{0,1},{1,2},{2,3},{4,5},{5,6},{6,7},{8,9},{9,10},{10,11},{12,13},{... | collective-permute-start | bytes 3538952 | tf_op jit(solution)/shard_map/ppermute | solution.py:20
  311.8 2.7 copy-start.5
  323.3 65.8 %all-to-all-start = ((bf16[8,2,98304]{2,1,0:T(2,128)(2,1)}), bf16[8,2,98304]{2,1,0:T(2,128)(2,1)S(1)}, u32[]{:S(2)}, u32[]{:S(2)}) async-start(bf16[8,2,98304]{2,1,0:T(2,128)(2,1)} %reshape.335), calls=%async_computation | async-start | bytes 6291456 | tf_op jit(solution)/shard_map/all_to_all | solution.py:87
  403.8 9.6 copy-start
  1305.9 8.6 copy-start.7
  1312.5 7.8 collective-permute-start.1
  1335.7 7.1 collective-permute-start.2
  1351.0 1.6 copy-start.3
  1351.4 1.9 copy-start.2
  1353.0 1.7 copy-start.1
  1359.1 7.7 collective-permute-start.3
  1368.3 1.6 copy-start.4
  1373.3 7.7 collective-permute-start.4
